TPU v7x, 32 devices: a whole 2x2x4 slice. The times are simulated.
32 devices in a mesh: grp: 4 (over z), shard: 8 (over y, x, core).
Axes of the slice: x: 2, y: 2, z: 4, core: 2. Of those that a mesh axis runs over, the one named last changes fastest.
Arguments:
- latents: bfloat16 [4096, 1024], P(('grp', 'shard')), may hold values from -6 to 6
- head_weight: bfloat16 [1024, 1024], P('shard'), may hold values from -0.1875 to 0.1875
- norm_gain: float32 [1024], replicated, may hold values from 0.1 to 1.9
- color_head: bfloat16 [4, 256], replicated, may hold values from -1.5 to 1.5
- sample_points: float32 [2048, 192], P(('grp', 'shard')), may hold values from -1 to 1
- sample_spacing: float32 [2048, 64], P(('grp', 'shard')), may hold values from 0.002 to 0.02
- ray_targets: float32 [3, 2048], P(None, ('grp', 'shard')), may hold values from 0 to 1
- ray_scene: int32 [2048], P(('grp', 'shard')), may hold values from 0 to 31, as said below
Outputs:
- rendered_color: float32 [3, 2048], P(None, ('grp', 'shard'))
- loss: float32 [], replicated
- head_grad: float32 [1024, 1024], P('shard')
- norm_gain_grad: float32 [1024], replicated
- latent_grad: bfloat16 [4096, 1024], P(('grp', 'shard'))
Inputs may be any that keep to these rules, and one draw needn't show every extreme that they name: `ray_scene`: one scene, drawn from the seed, is named by exactly 8 rays of every device; no device names any scene more than 8 times; every scene is named by one ray or more, and the totals of the other scenes differ from one another by one at most.
All inputs are finite; a program needn't handle non-finite values.
Results may differ from a plain program's by a relative error of at most 0.017.
Values may be sent and summed in bfloat16 or wider, within the bound.
A program may use at most 64 MiB of HBM per device.

v0:
```python
import math
import jax
import jax.numpy as jnp
from jax import lax
from jax.sharding import PartitionSpec as P

norm_eps = 1e-06


def encode(sample_rows, field_width):
    column = jnp.arange(field_width)
    component = column % 3
    octave = (column // 6 % 8).astype(jnp.float32)
    frequency = jnp.exp2(octave) * math.pi
    phase_shift = (column // 3 % 2).astype(jnp.float32) * (0.5 * math.pi)
    picked = jnp.zeros((sample_rows.shape[0], field_width), jnp.float32)
    for coord in range(3):
        chosen = (component == coord).astype(jnp.float32)
        picked = picked + sample_rows[:, coord : coord + 1] * chosen[None, :]
    return jnp.sin(picked * frequency + phase_shift)


def point_rows(points, ray_depth):
    ray_number = points.shape[0]
    return (
        points.reshape(ray_number, 3, ray_depth)
        .transpose(0, 2, 1)
        .reshape(ray_number * ray_depth, 3)
    )


def render_rays(points, spacing, target, live_rays, scene_factor, w_first, w_second, color_head):
    ray_number, ray_depth = spacing.shape
    field_width = w_first.shape[0]
    fan_scale = field_width ** (-0.5)
    sample_rows = point_rows(points, ray_depth)
    h_zero = encode(sample_rows, field_width).astype(jnp.bfloat16)
    h_one = jax.nn.relu(
        jnp.dot(h_zero, w_first, preferred_element_type=jnp.float32) * fan_scale
    ).astype(jnp.bfloat16)
    h_two = jax.nn.relu(
        jnp.dot(h_one, w_second, preferred_element_type=jnp.float32) * fan_scale
    ).astype(jnp.bfloat16)
    raw_out = lax.dot_general(
        color_head, h_two, (((1,), (1,)), ((), ())), preferred_element_type=jnp.float32
    )
    density = jax.nn.softplus(raw_out[0]).reshape(ray_number, ray_depth)
    albedo = jax.nn.sigmoid(raw_out[1:4]).reshape(3, ray_number, ray_depth)
    optical = density * spacing
    optical_before = jnp.cumsum(optical, axis=1) - optical
    transmit = jnp.exp(-optical_before)
    survive = jnp.exp(-optical)
    blend = transmit * (1.0 - survive)
    ray_color = jnp.sum(blend[None] * (albedo - 1.0), axis=2) + 1.0
    residual = ray_color - target.T
    loss_part = jnp.sum(
        jnp.where(live_rays, jnp.sum(residual * residual, axis=0) * scene_factor, 0.0)
    )
    grad_color = jnp.where(live_rays[None, :], 2.0 * residual * scene_factor, 0.0)
    d_albedo = grad_color[:, :, None] * blend[None]
    d_blend = jnp.sum(grad_color[:, :, None] * (albedo - 1.0), axis=0)
    weighted = d_blend * blend
    behind = jnp.sum(weighted, axis=1, keepdims=True) - jnp.cumsum(weighted, axis=1)
    d_optical = d_blend * transmit * survive - behind
    d_density = (
        d_optical * spacing * jax.nn.sigmoid(raw_out[0]).reshape(ray_number, ray_depth)
    ).reshape(1, ray_number * ray_depth)
    d_tint = (d_albedo * albedo * (1.0 - albedo)).reshape(3, ray_number * ray_depth)
    d_raw = jnp.concatenate([d_density, d_tint], axis=0).astype(jnp.bfloat16)
    d_htwo = lax.dot_general(
        d_raw, color_head, (((0,), (0,)), ((), ())), preferred_element_type=jnp.float32
    )
    d_atwo = (jnp.where(h_two > 0, d_htwo, 0.0) * fan_scale).astype(jnp.bfloat16)
    grad_second = lax.dot_general(
        h_one, d_atwo, (((0,), (0,)), ((), ())), preferred_element_type=jnp.float32
    )
    d_hone = lax.dot_general(
        d_atwo, w_second, (((1,), (1,)), ((), ())), preferred_element_type=jnp.float32
    )
    d_aone = (jnp.where(h_one > 0, d_hone, 0.0) * fan_scale).astype(jnp.bfloat16)
    grad_first = lax.dot_general(
        h_zero, d_aone, (((0,), (0,)), ((), ())), preferred_element_type=jnp.float32
    )
    return (ray_color, loss_part, grad_first, grad_second)


def body(
    latents,
    head_weight,
    norm_gain,
    color_head,
    sample_points,
    sample_spacing,
    ray_targets,
    ray_scene,
):
    devices = lax.axis_size(("grp", "shard"))
    ray_count, ray_depth = sample_spacing.shape
    tokens, model = latents.shape
    field_width = color_head.shape[1]
    per_layer = field_width * field_width // model
    per_device = 4 * ray_count // devices
    slot_total = per_device * devices
    latent_f32 = latents.astype(jnp.float32)
    inv_rms = lax.rsqrt(jnp.mean(latent_f32 * latent_f32, axis=1, keepdims=True) + norm_eps)
    x_hat = latent_f32 * inv_rms
    x_norm = (x_hat * norm_gain).astype(jnp.bfloat16)
    columns = x_norm
    field_sum = jnp.dot(
        columns,
        lax.all_gather(head_weight, "shard", axis=0, tiled=True),
        preferred_element_type=jnp.float32,
    )
    field_rows = field_sum.astype(jnp.bfloat16)
    w_first = field_rows[:per_layer].reshape(field_width, field_width)
    w_second = field_rows[per_layer:].reshape(field_width, field_width)
    ray_ids = jnp.arange(ray_count, dtype=jnp.int32)
    same_scene = ray_scene[:, None] == ray_scene[None, :]
    earlier = ray_ids[:, None] < ray_ids[None, :]
    ray_rank = jnp.sum(jnp.logical_and(same_scene, earlier).astype(jnp.int32), axis=0)
    slot_of_ray = ray_scene * per_device + ray_rank
    payload = jnp.concatenate([sample_points, sample_spacing], axis=1)
    send_payload = (
        jnp.zeros((slot_total, payload.shape[1]), jnp.float32).at[slot_of_ray].set(payload)
    )
    send_target = jnp.zeros((slot_total, 3), jnp.float32).at[slot_of_ray].set(ray_targets.T)
    send_live = jnp.zeros((slot_total,), jnp.float32).at[slot_of_ray].set(1.0)
    recv_payload, recv_target, recv_live = (
        lax.all_to_all(send_payload, ("grp", "shard"), split_axis=0, concat_axis=0, tiled=True),
        lax.all_to_all(send_target, ("grp", "shard"), split_axis=0, concat_axis=0, tiled=True),
        lax.all_to_all(send_live, ("grp", "shard"), split_axis=0, concat_axis=0, tiled=True),
    )
    block_rays = 1024 // ray_depth
    block_total = slot_total // block_rays
    scene_rays = jnp.sum(recv_live)
    scene_factor = 1.0 / (devices * scene_rays)

    def render_block(running, block_item):
        grad_first, grad_second, loss_sum = running
        block_payload, block_target, block_live = block_item
        ray_color, loss_part, more_first, more_second = render_rays(
            block_payload[:, : 3 * ray_depth],
            block_payload[:, 3 * ray_depth :],
            block_target,
            block_live > 0.5,
            scene_factor,
            w_first,
            w_second,
            color_head,
        )
        return (
            (grad_first + more_first, grad_second + more_second, loss_sum + loss_part),
            ray_color,
        )

    zero_grad = jnp.zeros((field_width, field_width), jnp.float32)
    block_items = (
        recv_payload.reshape(block_total, block_rays, payload.shape[1]),
        recv_target.reshape(block_total, block_rays, 3),
        recv_live.reshape(block_total, block_rays),
    )
    (grad_first, grad_second, loss_sum), block_colors = lax.scan(
        render_block, (zero_grad, zero_grad, jnp.zeros((), jnp.float32)), block_items
    )
    slot_colors = block_colors.transpose(1, 0, 2).reshape(3, slot_total)
    returned = lax.all_to_all(
        slot_colors, ("grp", "shard"), split_axis=1, concat_axis=1, tiled=True
    )
    rendered = returned[:, slot_of_ray]
    d_field = jnp.concatenate(
        [grad_first.reshape(per_layer, model), grad_second.reshape(per_layer, model)], axis=0
    ).astype(jnp.bfloat16)
    d_norm = lax.dot_general(
        d_field,
        lax.all_gather(head_weight, "shard", axis=0, tiled=True),
        (((1,), (1,)), ((), ())),
        preferred_element_type=jnp.float32,
    )
    columns = x_norm
    group_part = lax.psum_scatter(
        lax.dot_general(
            columns, d_field, (((0,), (0,)), ((), ())), preferred_element_type=jnp.float32
        ).astype(jnp.bfloat16),
        "shard",
        scatter_dimension=0,
        tiled=True,
    )
    head_grad = lax.psum(group_part, "grp").astype(jnp.float32)
    gain_part = jnp.sum(d_norm * x_hat, axis=0)
    norm_gain_grad, loss_total = lax.psum((gain_part, loss_sum), ("grp", "shard"))
    d_scaled = d_norm * norm_gain
    latent_grad = (
        inv_rms * (d_scaled - x_hat * jnp.mean(d_scaled * x_hat, axis=1, keepdims=True))
    ).astype(jnp.bfloat16)
    return (rendered, loss_total, head_grad, norm_gain_grad, latent_grad)


def solution(mesh):
    placed = (
        P(("grp", "shard"), None),
        P("shard", None),
        P(),
        P(),
        P(("grp", "shard"), None),
        P(("grp", "shard"), None),
        P(None, ("grp", "shard")),
        P(("grp", "shard")),
    )
    return jax.shard_map(
        body,
        mesh=mesh,
        in_specs=placed,
        out_specs=(
            P(None, ("grp", "shard")),
            P(),
            P("shard", None),
            P(),
            P(("grp", "shard"), None),
        ),
        check_vma=False,
    )
```

profile of v0, /device:TPU:0, one launch (start us, length us, event | category | flops | bytes accessed | tf_op | source)
XLA Modules:
  0.0 360.1 jit_solution(17849473619523795206)
XLA Ops:
  7.2 0.7 all-gather.2.cloned.1.call-update
  7.9 0.8 convert_reduce_fusion
  8.7 0.7 compare_select_fusion.5
  9.4 0.8 scatter_custom_fusion.1
  10.2 0.7 all_to_all.28
  10.9 7.3 %all-to-all-start.1 = ((f32[32,8,1]{1,2,0:T(1,128)}), f32[32,8,1]{1,2,0:T(1,128)S(1)}, u32[]{:S(2)}, u32[]{:S(2)}) async-start(f32[32,8,1]{1,2,0:T(1,128)} %bitcast.2), calls=%async_computation.1 | async-start | bytes 32768 | tf_op jit(solution)/shard_map/all_to_all | solution.py:131
  18.2 1.1 fusion.46
  19.3 0.8 copy.34
  20.1 0.8 scatter_custom_fusion.2
  20.9 0.9 copy.35
  21.8 1.9 scatter_custom_fusion
  23.6 1.7 all-to-all-done.1
  25.4 4.1 %all-to-all-start.2 = ((f32[32,8,3]{1,2,0:T(4,128)}), f32[32,8,3]{1,2,0:T(4,128)S(1)}, u32[]{:S(2)}, u32[]{:S(2)}) async-start(f32[32,8,3]{1,2,0:T(4,128)} %copy.35), calls=%async_computation.2 | async-start | bytes 131072 | tf_op jit(solution)/shard_map/all_to_all | solution.py:130
  30.0 1.3 fusion.59
  32.1 4.9 %all-to-all-done.2 = f32[32,8,3]{1,2,0:T(4,128)S(1)} async-done(((f32[32,8,3]{1,2,0:T(4,128)}), f32[32,8,3]{1,2,0:T(4,128)S(1)}, u32[]{:S(2)}, u32[]{:S(2)}) %all-to-all-start.2) | async-done | bytes 3104 | tf_op jit(solution)/shard_map/all_to_all | solution.py:130
  37.0 2.7 all-to-all-start
  39.9 1.2 all-gather.2.cloned.1.call-done
  41.1 2.1 convolution_convert_fusion.1
  43.4 6.9 %all-to-all-done = f32[32,8,256]{2,1,0:T(8,128)S(1)} async-done(((f32[32,8,256]{2,1,0:T(8,128)}), f32[32,8,256]{2,1,0:T(8,128)S(1)}, u32[]{:S(2)}, u32[]{:S(2)}) %all-to-all-start) | async-done | bytes 262176 | tf_op jit(solution)/shard_map/all_to_all | solution.py:129
  50.3 210.9 %while.20 = (s32[]{:T(128)}, f32[256,256]{1,0:T(8,128)S(1)}, f32[256,256]{1,0:T(8,128)S(1)}, f32[]{:T(128)}, f32[16,3,16]{2,1,0:T(4,128)S(1)}, /*index=5*/f32[16...) while((s32[]{:T(128)}, f32[256,256]{1,0:T(8,128)S(1)}, ...), condition=%wide.region_14.15_spmd.clone, body=%wide.region_6.14_spmd.clone.sunk | while | flops 683649216 | bytes 7148784 | solution.py:162
  50.6 4.6 %fusion.109 = bf16[1024,256]{1,0:T(8,128)(2,1)S(1)} fusion(bf16[256,256]{1,0:T(8,128)(2,1)S(1)} %get-tuple-element.516, f32[256]{0:T(256)S(1)} %get-tuple-element.465, f32[256]{0:T(256)S(1)} %get-tuple-element.466, f32[256]{0:T(256)S(1)} %get-tuple-element.467, f32[1024]{0:T(1024)S(1)} %bitcast.98, f32[256]{0:T(256)S(1)} %get-tuple-element.469, ...), kind=kOutput, calls=%fused_computation.12.clone.1 | convolution fusion | flops 137101312 | bytes 672768 | tf_op jit(solution)/shard_map/while/body/eval_jaxpr/dot_general | solution.py:39
  56.3 0.6 select_reduce_fusion.2
  58.6 4.2 %fusion.114 = f32[256,256]{1,0:T(8,128)S(1)} fusion(bf16[1024,256]{1,0:T(8,128)(2,1)S(1)} %fusion.113, bf16[256,256]{1,0:T(8,128)(2,1)S(1)} %get-tuple-element.517, bf16[1024,256]{1,0:T(8,128)(2,1)S(1)} %fusion.109, f32[256,256]{1,0:T(8,128)S(1)} %get-tuple-element.495, f32[256]{0:T(256)S(1)} %get-tuple-element.465, f32[256]{0:T(256)S(1)} %get-tuple-element.466, ...), kind=kOutput, calls=%fused_computation.17.clone.1 | convolution fusion | flops 271712256 | bytes 1721345 | tf_op jit(solution)/shard_map/while/body/eval_jaxpr/dot_general | solution.py:81
  63.8 4.6 %fusion.109 = bf16[1024,256]{1,0:T(8,128)(2,1)S(1)} fusion(bf16[256,256]{1,0:T(8,128)(2,1)S(1)} %get-tuple-element.516, f32[256]{0:T(256)S(1)} %get-tuple-element.465, f32[256]{0:T(256)S(1)} %get-tuple-element.466, f32[256]{0:T(256)S(1)} %get-tuple-element.467, f32[1024]{0:T(1024)S(1)} %bitcast.98, f32[256]{0:T(256)S(1)} %get-tuple-element.469, ...), kind=kOutput, calls=%fused_computation.12.clone.1 | convolution fusion | flops 137101312 | bytes 672768 | tf_op jit(solution)/shard_map/while/body/eval_jaxpr/dot_general | solution.py:39
  69.5 0.6 select_reduce_fusion.2
  71.8 4.2 %fusion.114 = f32[256,256]{1,0:T(8,128)S(1)} fusion(bf16[1024,256]{1,0:T(8,128)(2,1)S(1)} %fusion.113, bf16[256,256]{1,0:T(8,128)(2,1)S(1)} %get-tuple-element.517, bf16[1024,256]{1,0:T(8,128)(2,1)S(1)} %fusion.109, f32[256,256]{1,0:T(8,128)S(1)} %get-tuple-element.495, f32[256]{0:T(256)S(1)} %get-tuple-element.465, f32[256]{0:T(256)S(1)} %get-tuple-element.466, ...), kind=kOutput, calls=%fused_computation.17.clone.1 | convolution fusion | flops 271712256 | bytes 1721345 | tf_op jit(solution)/shard_map/while/body/eval_jaxpr/dot_general | solution.py:81
  76.9 4.6 %fusion.109 = bf16[1024,256]{1,0:T(8,128)(2,1)S(1)} fusion(bf16[256,256]{1,0:T(8,128)(2,1)S(1)} %get-tuple-element.516, f32[256]{0:T(256)S(1)} %get-tuple-element.465, f32[256]{0:T(256)S(1)} %get-tuple-element.466, f32[256]{0:T(256)S(1)} %get-tuple-element.467, f32[1024]{0:T(1024)S(1)} %bitcast.98, f32[256]{0:T(256)S(1)} %get-tuple-element.469, ...), kind=kOutput, calls=%fused_computation.12.clone.1 | convolution fusion | flops 137101312 | bytes 672768 | tf_op jit(solution)/shard_map/while/body/eval_jaxpr/dot_general | solution.py:39
  82.7 0.6 select_reduce_fusion.2
  85.0 4.2 %fusion.114 = f32[256,256]{1,0:T(8,128)S(1)} fusion(bf16[1024,256]{1,0:T(8,128)(2,1)S(1)} %fusion.113, bf16[256,256]{1,0:T(8,128)(2,1)S(1)} %get-tuple-element.517, bf16[1024,256]{1,0:T(8,128)(2,1)S(1)} %fusion.109, f32[256,256]{1,0:T(8,128)S(1)} %get-tuple-element.495, f32[256]{0:T(256)S(1)} %get-tuple-element.465, f32[256]{0:T(256)S(1)} %get-tuple-element.466, ...), kind=kOutput, calls=%fused_computation.17.clone.1 | convolution fusion | flops 271712256 | bytes 1721345 | tf_op jit(solution)/shard_map/while/body/eval_jaxpr/dot_general | solution.py:81
  90.1 4.6 %fusion.109 = bf16[1024,256]{1,0:T(8,128)(2,1)S(1)} fusion(bf16[256,256]{1,0:T(8,128)(2,1)S(1)} %get-tuple-element.516, f32[256]{0:T(256)S(1)} %get-tuple-element.465, f32[256]{0:T(256)S(1)} %get-tuple-element.466, f32[256]{0:T(256)S(1)} %get-tuple-element.467, f32[1024]{0:T(1024)S(1)} %bitcast.98, f32[256]{0:T(256)S(1)} %get-tuple-element.469, ...), kind=kOutput, calls=%fused_computation.12.clone.1 | convolution fusion | flops 137101312 | bytes 672768 | tf_op jit(solution)/shard_map/while/body/eval_jaxpr/dot_general | solution.py:39
  98.2 4.2 %fusion.114 = f32[256,256]{1,0:T(8,128)S(1)} fusion(bf16[1024,256]{1,0:T(8,128)(2,1)S(1)} %fusion.113, bf16[256,256]{1,0:T(8,128)(2,1)S(1)} %get-tuple-element.517, bf16[1024,256]{1,0:T(8,128)(2,1)S(1)} %fusion.109, f32[256,256]{1,0:T(8,128)S(1)} %get-tuple-element.495, f32[256]{0:T(256)S(1)} %get-tuple-element.465, f32[256]{0:T(256)S(1)} %get-tuple-element.466, ...), kind=kOutput, calls=%fused_computation.17.clone.1 | convolution fusion | flops 271712256 | bytes 1721345 | tf_op jit(solution)/shard_map/while/body/eval_jaxpr/dot_general | solution.py:81
  103.3 4.6 %fusion.109 = bf16[1024,256]{1,0:T(8,128)(2,1)S(1)} fusion(bf16[256,256]{1,0:T(8,128)(2,1)S(1)} %get-tuple-element.516, f32[256]{0:T(256)S(1)} %get-tuple-element.465, f32[256]{0:T(256)S(1)} %get-tuple-element.466, f32[256]{0:T(256)S(1)} %get-tuple-element.467, f32[1024]{0:T(1024)S(1)} %bitcast.98, f32[256]{0:T(256)S(1)} %get-tuple-element.469, ...), kind=kOutput, calls=%fused_computation.12.clone.1 | convolution fusion | flops 137101312 | bytes 672768 | tf_op jit(solution)/shard_map/while/body/eval_jaxpr/dot_general | solution.py:39
  111.3 4.2 %fusion.114 = f32[256,256]{1,0:T(8,128)S(1)} fusion(bf16[1024,256]{1,0:T(8,128)(2,1)S(1)} %fusion.113, bf16[256,256]{1,0:T(8,128)(2,1)S(1)} %get-tuple-element.517, bf16[1024,256]{1,0:T(8,128)(2,1)S(1)} %fusion.109, f32[256,256]{1,0:T(8,128)S(1)} %get-tuple-element.495, f32[256]{0:T(256)S(1)} %get-tuple-element.465, f32[256]{0:T(256)S(1)} %get-tuple-element.466, ...), kind=kOutput, calls=%fused_computation.17.clone.1 | convolution fusion | flops 271712256 | bytes 1721345 | tf_op jit(solution)/shard_map/while/body/eval_jaxpr/dot_general | solution.py:81
  116.5 4.6 %fusion.109 = bf16[1024,256]{1,0:T(8,128)(2,1)S(1)} fusion(bf16[256,256]{1,0:T(8,128)(2,1)S(1)} %get-tuple-element.516, f32[256]{0:T(256)S(1)} %get-tuple-element.465, f32[256]{0:T(256)S(1)} %get-tuple-element.466, f32[256]{0:T(256)S(1)} %get-tuple-element.467, f32[1024]{0:T(1024)S(1)} %bitcast.98, f32[256]{0:T(256)S(1)} %get-tuple-element.469, ...), kind=kOutput, calls=%fused_computation.12.clone.1 | convolution fusion | flops 137101312 | bytes 672768 | tf_op jit(solution)/shard_map/while/body/eval_jaxpr/dot_general | solution.py:39
  124.5 4.2 %fusion.114 = f32[256,256]{1,0:T(8,128)S(1)} fusion(bf16[1024,256]{1,0:T(8,128)(2,1)S(1)} %fusion.113, bf16[256,256]{1,0:T(8,128)(2,1)S(1)} %get-tuple-element.517, bf16[1024,256]{1,0:T(8,128)(2,1)S(1)} %fusion.109, f32[256,256]{1,0:T(8,128)S(1)} %get-tuple-element.495, f32[256]{0:T(256)S(1)} %get-tuple-element.465, f32[256]{0:T(256)S(1)} %get-tuple-element.466, ...), kind=kOutput, calls=%fused_computation.17.clone.1 | convolution fusion | flops 271712256 | bytes 1721345 | tf_op jit(solution)/shard_map/while/body/eval_jaxpr/dot_general | solution.py:81
  129.7 4.6 %fusion.109 = bf16[1024,256]{1,0:T(8,128)(2,1)S(1)} fusion(bf16[256,256]{1,0:T(8,128)(2,1)S(1)} %get-tuple-element.516, f32[256]{0:T(256)S(1)} %get-tuple-element.465, f32[256]{0:T(256)S(1)} %get-tuple-element.466, f32[256]{0:T(256)S(1)} %get-tuple-element.467, f32[1024]{0:T(1024)S(1)} %bitcast.98, f32[256]{0:T(256)S(1)} %get-tuple-element.469, ...), kind=kOutput, calls=%fused_computation.12.clone.1 | convolution fusion | flops 137101312 | bytes 672768 | tf_op jit(solution)/shard_map/while/body/eval_jaxpr/dot_general | solution.py:39
  137.7 4.2 %fusion.114 = f32[256,256]{1,0:T(8,128)S(1)} fusion(bf16[1024,256]{1,0:T(8,128)(2,1)S(1)} %fusion.113, bf16[256,256]{1,0:T(8,128)(2,1)S(1)} %get-tuple-element.517, bf16[1024,256]{1,0:T(8,128)(2,1)S(1)} %fusion.109, f32[256,256]{1,0:T(8,128)S(1)} %get-tuple-element.495, f32[256]{0:T(256)S(1)} %get-tuple-element.465, f32[256]{0:T(256)S(1)} %get-tuple-element.466, ...), kind=kOutput, calls=%fused_computation.17.clone.1 | convolution fusion | flops 271712256 | bytes 1721345 | tf_op jit(solution)/shard_map/while/body/eval_jaxpr/dot_general | solution.py:81
  142.8 4.6 %fusion.109 = bf16[1024,256]{1,0:T(8,128)(2,1)S(1)} fusion(bf16[256,256]{1,0:T(8,128)(2,1)S(1)} %get-tuple-element.516, f32[256]{0:T(256)S(1)} %get-tuple-element.465, f32[256]{0:T(256)S(1)} %get-tuple-element.466, f32[256]{0:T(256)S(1)} %get-tuple-element.467, f32[1024]{0:T(1024)S(1)} %bitcast.98, f32[256]{0:T(256)S(1)} %get-tuple-element.469, ...), kind=kOutput, calls=%fused_computation.12.clone.1 | convolution fusion | flops 137101312 | bytes 672768 | tf_op jit(solution)/shard_map/while/body/eval_jaxpr/dot_general | solution.py:39
  150.9 4.2 %fusion.114 = f32[256,256]{1,0:T(8,128)S(1)} fusion(bf16[1024,256]{1,0:T(8,128)(2,1)S(1)} %fusion.113, bf16[256,256]{1,0:T(8,128)(2,1)S(1)} %get-tuple-element.517, bf16[1024,256]{1,0:T(8,128)(2,1)S(1)} %fusion.109, f32[256,256]{1,0:T(8,128)S(1)} %get-tuple-element.495, f32[256]{0:T(256)S(1)} %get-tuple-element.465, f32[256]{0:T(256)S(1)} %get-tuple-element.466, ...), kind=kOutput, calls=%fused_computation.17.clone.1 | convolution fusion | flops 271712256 | bytes 1721345 | tf_op jit(solution)/shard_map/while/body/eval_jaxpr/dot_general | solution.py:81
  156.0 4.6 %fusion.109 = bf16[1024,256]{1,0:T(8,128)(2,1)S(1)} fusion(bf16[256,256]{1,0:T(8,128)(2,1)S(1)} %get-tuple-element.516, f32[256]{0:T(256)S(1)} %get-tuple-element.465, f32[256]{0:T(256)S(1)} %get-tuple-element.466, f32[256]{0:T(256)S(1)} %get-tuple-element.467, f32[1024]{0:T(1024)S(1)} %bitcast.98, f32[256]{0:T(256)S(1)} %get-tuple-element.469, ...), kind=kOutput, calls=%fused_computation.12.clone.1 | convolution fusion | flops 137101312 | bytes 672768 | tf_op jit(solution)/shard_map/while/body/eval_jaxpr/dot_general | solution.py:39
  164.1 4.2 %fusion.114 = f32[256,256]{1,0:T(8,128)S(1)} fusion(bf16[1024,256]{1,0:T(8,128)(2,1)S(1)} %fusion.113, bf16[256,256]{1,0:T(8,128)(2,1)S(1)} %get-tuple-element.517, bf16[1024,256]{1,0:T(8,128)(2,1)S(1)} %fusion.109, f32[256,256]{1,0:T(8,128)S(1)} %get-tuple-element.495, f32[256]{0:T(256)S(1)} %get-tuple-element.465, f32[256]{0:T(256)S(1)} %get-tuple-element.466, ...), kind=kOutput, calls=%fused_computation.17.clone.1 | convolution fusion | flops 271712256 | bytes 1721345 | tf_op jit(solution)/shard_map/while/body/eval_jaxpr/dot_general | solution.py:81
  169.2 4.6 %fusion.109 = bf16[1024,256]{1,0:T(8,128)(2,1)S(1)} fusion(bf16[256,256]{1,0:T(8,128)(2,1)S(1)} %get-tuple-element.516, f32[256]{0:T(256)S(1)} %get-tuple-element.465, f32[256]{0:T(256)S(1)} %get-tuple-element.466, f32[256]{0:T(256)S(1)} %get-tuple-element.467, f32[1024]{0:T(1024)S(1)} %bitcast.98, f32[256]{0:T(256)S(1)} %get-tuple-element.469, ...), kind=kOutput, calls=%fused_computation.12.clone.1 | convolution fusion | flops 137101312 | bytes 672768 | tf_op jit(solution)/shard_map/while/body/eval_jaxpr/dot_general | solution.py:39
  177.2 4.2 %fusion.114 = f32[256,256]{1,0:T(8,128)S(1)} fusion(bf16[1024,256]{1,0:T(8,128)(2,1)S(1)} %fusion.113, bf16[256,256]{1,0:T(8,128)(2,1)S(1)} %get-tuple-element.517, bf16[1024,256]{1,0:T(8,128)(2,1)S(1)} %fusion.109, f32[256,256]{1,0:T(8,128)S(1)} %get-tuple-element.495, f32[256]{0:T(256)S(1)} %get-tuple-element.465, f32[256]{0:T(256)S(1)} %get-tuple-element.466, ...), kind=kOutput, calls=%fused_computation.17.clone.1 | convolution fusion | flops 271712256 | bytes 1721345 | tf_op jit(solution)/shard_map/while/body/eval_jaxpr/dot_general | solution.py:81
  182.4 4.6 %fusion.109 = bf16[1024,256]{1,0:T(8,128)(2,1)S(1)} fusion(bf16[256,256]{1,0:T(8,128)(2,1)S(1)} %get-tuple-element.516, f32[256]{0:T(256)S(1)} %get-tuple-element.465, f32[256]{0:T(256)S(1)} %get-tuple-element.466, f32[256]{0:T(256)S(1)} %get-tuple-element.467, f32[1024]{0:T(1024)S(1)} %bitcast.98, f32[256]{0:T(256)S(1)} %get-tuple-element.469, ...), kind=kOutput, calls=%fused_computation.12.clone.1 | convolution fusion | flops 137101312 | bytes 672768 | tf_op jit(solution)/shard_map/while/body/eval_jaxpr/dot_general | solution.py:39
  190.4 4.2 %fusion.114 = f32[256,256]{1,0:T(8,128)S(1)} fusion(bf16[1024,256]{1,0:T(8,128)(2,1)S(1)} %fusion.113, bf16[256,256]{1,0:T(8,128)(2,1)S(1)} %get-tuple-element.517, bf16[1024,256]{1,0:T(8,128)(2,1)S(1)} %fusion.109, f32[256,256]{1,0:T(8,128)S(1)} %get-tuple-element.495, f32[256]{0:T(256)S(1)} %get-tuple-element.465, f32[256]{0:T(256)S(1)} %get-tuple-element.466, ...), kind=kOutput, calls=%fused_computation.17.clone.1 | convolution fusion | flops 271712256 | bytes 1721345 | tf_op jit(solution)/shard_map/while/body/eval_jaxpr/dot_general | solution.py:81
  195.6 4.6 %fusion.109 = bf16[1024,256]{1,0:T(8,128)(2,1)S(1)} fusion(bf16[256,256]{1,0:T(8,128)(2,1)S(1)} %get-tuple-element.516, f32[256]{0:T(256)S(1)} %get-tuple-element.465, f32[256]{0:T(256)S(1)} %get-tuple-element.466, f32[256]{0:T(256)S(1)} %get-tuple-element.467, f32[1024]{0:T(1024)S(1)} %bitcast.98, f32[256]{0:T(256)S(1)} %get-tuple-element.469, ...), kind=kOutput, calls=%fused_computation.12.clone.1 | convolution fusion | flops 137101312 | bytes 672768 | tf_op jit(solution)/shard_map/while/body/eval_jaxpr/dot_general | solution.py:39
  203.6 4.2 %fusion.114 = f32[256,256]{1,0:T(8,128)S(1)} fusion(bf16[1024,256]{1,0:T(8,128)(2,1)S(1)} %fusion.113, bf16[256,256]{1,0:T(8,128)(2,1)S(1)} %get-tuple-element.517, bf16[1024,256]{1,0:T(8,128)(2,1)S(1)} %fusion.109, f32[256,256]{1,0:T(8,128)S(1)} %get-tuple-element.495, f32[256]{0:T(256)S(1)} %get-tuple-element.465, f32[256]{0:T(256)S(1)} %get-tuple-element.466, ...), kind=kOutput, calls=%fused_computation.17.clone.1 | convolution fusion | flops 271712256 | bytes 1721345 | tf_op jit(solution)/shard_map/while/body/eval_jaxpr/dot_general | solution.py:81
  208.8 4.6 %fusion.109 = bf16[1024,256]{1,0:T(8,128)(2,1)S(1)} fusion(bf16[256,256]{1,0:T(8,128)(2,1)S(1)} %get-tuple-element.516, f32[256]{0:T(256)S(1)} %get-tuple-element.465, f32[256]{0:T(256)S(1)} %get-tuple-element.466, f32[256]{0:T(256)S(1)} %get-tuple-element.467, f32[1024]{0:T(1024)S(1)} %bitcast.98, f32[256]{0:T(256)S(1)} %get-tuple-element.469, ...), kind=kOutput, calls=%fused_computation.12.clone.1 | convolution fusion | flops 137101312 | bytes 672768 | tf_op jit(solution)/shard_map/while/body/eval_jaxpr/dot_general | solution.py:39
  216.8 4.2 %fusion.114 = f32[256,256]{1,0:T(8,128)S(1)} fusion(bf16[1024,256]{1,0:T(8,128)(2,1)S(1)} %fusion.113, bf16[256,256]{1,0:T(8,128)(2,1)S(1)} %get-tuple-element.517, bf16[1024,256]{1,0:T(8,128)(2,1)S(1)} %fusion.109, f32[256,256]{1,0:T(8,128)S(1)} %get-tuple-element.495, f32[256]{0:T(256)S(1)} %get-tuple-element.465, f32[256]{0:T(256)S(1)} %get-tuple-element.466, ...), kind=kOutput, calls=%fused_computation.17.clone.1 | convolution fusion | flops 271712256 | bytes 1721345 | tf_op jit(solution)/shard_map/while/body/eval_jaxpr/dot_general | solution.py:81
  221.9 4.6 %fusion.109 = bf16[1024,256]{1,0:T(8,128)(2,1)S(1)} fusion(bf16[256,256]{1,0:T(8,128)(2,1)S(1)} %get-tuple-element.516, f32[256]{0:T(256)S(1)} %get-tuple-element.465, f32[256]{0:T(256)S(1)} %get-tuple-element.466, f32[256]{0:T(256)S(1)} %get-tuple-element.467, f32[1024]{0:T(1024)S(1)} %bitcast.98, f32[256]{0:T(256)S(1)} %get-tuple-element.469, ...), kind=kOutput, calls=%fused_computation.12.clone.1 | convolution fusion | flops 137101312 | bytes 672768 | tf_op jit(solution)/shard_map/while/body/eval_jaxpr/dot_general | solution.py:39
  230.0 4.2 %fusion.114 = f32[256,256]{1,0:T(8,128)S(1)} fusion(bf16[1024,256]{1,0:T(8,128)(2,1)S(1)} %fusion.113, bf16[256,256]{1,0:T(8,128)(2,1)S(1)} %get-tuple-element.517, bf16[1024,256]{1,0:T(8,128)(2,1)S(1)} %fusion.109, f32[256,256]{1,0:T(8,128)S(1)} %get-tuple-element.495, f32[256]{0:T(256)S(1)} %get-tuple-element.465, f32[256]{0:T(256)S(1)} %get-tuple-element.466, ...), kind=kOutput, calls=%fused_computation.17.clone.1 | convolution fusion | flops 271712256 | bytes 1721345 | tf_op jit(solution)/shard_map/while/body/eval_jaxpr/dot_general | solution.py:81
  235.1 4.6 %fusion.109 = bf16[1024,256]{1,0:T(8,128)(2,1)S(1)} fusion(bf16[256,256]{1,0:T(8,128)(2,1)S(1)} %get-tuple-element.516, f32[256]{0:T(256)S(1)} %get-tuple-element.465, f32[256]{0:T(256)S(1)} %get-tuple-element.466, f32[256]{0:T(256)S(1)} %get-tuple-element.467, f32[1024]{0:T(1024)S(1)} %bitcast.98, f32[256]{0:T(256)S(1)} %get-tuple-element.469, ...), kind=kOutput, calls=%fused_computation.12.clone.1 | convolution fusion | flops 137101312 | bytes 672768 | tf_op jit(solution)/shard_map/while/body/eval_jaxpr/dot_general | solution.py:39
  243.2 4.2 %fusion.114 = f32[256,256]{1,0:T(8,128)S(1)} fusion(bf16[1024,256]{1,0:T(8,128)(2,1)S(1)} %fusion.113, bf16[256,256]{1,0:T(8,128)(2,1)S(1)} %get-tuple-element.517, bf16[1024,256]{1,0:T(8,128)(2,1)S(1)} %fusion.109, f32[256,256]{1,0:T(8,128)S(1)} %get-tuple-element.495, f32[256]{0:T(256)S(1)} %get-tuple-element.465, f32[256]{0:T(256)S(1)} %get-tuple-element.466, ...), kind=kOutput, calls=%fused_computation.17.clone.1 | convolution fusion | flops 271712256 | bytes 1721345 | tf_op jit(solution)/shard_map/while/body/eval_jaxpr/dot_general | solution.py:81
  248.3 4.6 %fusion.109 = bf16[1024,256]{1,0:T(8,128)(2,1)S(1)} fusion(bf16[256,256]{1,0:T(8,128)(2,1)S(1)} %get-tuple-element.516, f32[256]{0:T(256)S(1)} %get-tuple-element.465, f32[256]{0:T(256)S(1)} %get-tuple-element.466, f32[256]{0:T(256)S(1)} %get-tuple-element.467, f32[1024]{0:T(1024)S(1)} %bitcast.98, f32[256]{0:T(256)S(1)} %get-tuple-element.469, ...), kind=kOutput, calls=%fused_computation.12.clone.1 | convolution fusion | flops 137101312 | bytes 672768 | tf_op jit(solution)/shard_map/while/body/eval_jaxpr/dot_general | solution.py:39
  256.3 4.2 %fusion.114 = f32[256,256]{1,0:T(8,128)S(1)} fusion(bf16[1024,256]{1,0:T(8,128)(2,1)S(1)} %fusion.113, bf16[256,256]{1,0:T(8,128)(2,1)S(1)} %get-tuple-element.517, bf16[1024,256]{1,0:T(8,128)(2,1)S(1)} %fusion.109, f32[256,256]{1,0:T(8,128)S(1)} %get-tuple-element.495, f32[256]{0:T(256)S(1)} %get-tuple-element.465, f32[256]{0:T(256)S(1)} %get-tuple-element.466, ...), kind=kOutput, calls=%fused_computation.17.clone.1 | convolution fusion | flops 271712256 | bytes 1721345 | tf_op jit(solution)/shard_map/while/body/eval_jaxpr/dot_general | solution.py:81
  261.5 2.1 convolution_convert_fusion
  263.7 0.9 fusion.42
  264.7 38.0 %reduce-scatter.2.cloned.1.call-done = bf16[128,1024]{1,0:T(8,128)(2,1)} async-done(((bf16[1024,1024]{1,0:T(8,128)(2,1)}), bf16[128,1024]{1,0:T(8,128)(2,1)}) %reduce-scatter.2.cloned.1.call-update) | async-done | bytes 262160 | tf_op jit(solution)/shard_map/reduce_scatter | solution.py:180
  302.8 0.7 copy.39
  303.4 4.6 %all-to-all-start.3 = ((f32[3,32,8]{2,0,1:T(4,128)}), f32[3,32,8]{2,0,1:T(4,128)S(1)}, u32[]{:S(2)}, u32[]{:S(2)}) async-start(f32[3,32,8]{2,0,1:T(4,128)} %copy.39), calls=%async_computation.3 | async-start | bytes 131072 | tf_op jit(solution)/shard_map/all_to_all | solution.py:166
  308.0 0.9 fusion.45
  308.9 41.4 %all-reduce = (f32[]{:T(128)}, f32[1024]{0:T(1024)}) all-reduce(f32[]{:T(128)} %get-tuple-element.221, f32[1024]{0:T(1024)S(1)} %get-tuple-element.326), channel_id=1, replica_groups=mesh['grp'=4,'shard'=8] {'grp','shard'}, use_global_device_ids=true, to_apply=%region_15.16 | all-reduce | flops 1025 | bytes 8200 | tf_op jit(solution)/shard_map/psum | solution.py:190
  351.2 0.7 copy.41
  351.8 1.8 convert_element_type.122
  (580 shorter events, 58.6 us)
Async XLA Ops:
  7.2 33.9 %copy-start.1 = (bf16[128,1024]{1,0:T(8,128)(2,1)S(1)}, bf16[128,1024]{1,0:T(8,128)(2,1)}, u32[]{:S(2)}) copy-start(bf16[128,1024]{1,0:T(8,128)(2,1)} %param.10) | copy-start | bytes 786436
  7.2 33.9 %copy-start.2 = (f32[1024]{0:T(1024)S(1)}, f32[1024]{0:T(1024)}, u32[]{:S(2)}) copy-start(f32[1024]{0:T(1024)} %param.12) | copy-start | bytes 12292
  7.2 33.9 %all-gather.2.cloned.1.call-start = ((), (), s32[]{:S(2)}) async-start(), calls=%async_computation.5 | async-start | bytes 2359296 | tf_op jit(solution)/shard_map/all_gather | solution.py:111
  10.9 14.5 %all-to-all-start.1 = ((f32[32,8,1]{1,2,0:T(1,128)}), f32[32,8,1]{1,2,0:T(1,128)S(1)}, u32[]{:S(2)}, u32[]{:S(2)}) async-start(f32[32,8,1]{1,2,0:T(1,128)} %bitcast.2), calls=%async_computation.1 | async-start | bytes 32768 | tf_op jit(solution)/shard_map/all_to_all | solution.py:131
  25.4 11.6 %all-to-all-start.2 = ((f32[32,8,3]{1,2,0:T(4,128)}), f32[32,8,3]{1,2,0:T(4,128)S(1)}, u32[]{:S(2)}, u32[]{:S(2)}) async-start(f32[32,8,3]{1,2,0:T(4,128)} %copy.35), calls=%async_computation.2 | async-start | bytes 131072 | tf_op jit(solution)/shard_map/all_to_all | solution.py:130
  37.0 13.3 %copy-start.3 = (bf16[4,256]{1,0:T(4,128)(2,1)S(1)}, bf16[4,256]{1,0:T(4,128)(2,1)}, u32[]{:S(2)}) copy-start(bf16[4,256]{1,0:T(4,128)(2,1)} %param.13) | copy-start | bytes 6148
  37.0 13.3 %all-to-all-start = ((f32[32,8,256]{2,1,0:T(8,128)}), f32[32,8,256]{2,1,0:T(8,128)S(1)}, u32[]{:S(2)}, u32[]{:S(2)}) async-start(f32[32,8,256]{2,1,0:T(8,128)} %bitcast), calls=%async_computation | async-start | bytes 524288 | tf_op jit(solution)/shard_map/all_to_all | solution.py:129
  39.7 262.9 %reduce-scatter.2.cloned.1.call-start = ((), (), s32[]{:S(2)}) async-start(), calls=%async_computation.6 | async-start | bytes 2359296 | tf_op jit(solution)/shard_map/reduce_scatter | solution.py:180
  261.5 2.2 copy-start
  263.7 88.2 %all-reduce.3.cloned.1.call-start = ((), (), s32[]{:S(2)}) async-start(), calls=%async_computation.7 | async-start | bytes 524288 | tf_op jit(solution)/shard_map/psum | solution.py:188
  303.4 46.9 %all-to-all-start.3 = ((f32[3,32,8]{2,0,1:T(4,128)}), f32[3,32,8]{2,0,1:T(4,128)S(1)}, u32[]{:S(2)}, u32[]{:S(2)}) async-start(f32[3,32,8]{2,0,1:T(4,128)} %copy.39), calls=%async_computation.3 | async-start | bytes 131072 | tf_op jit(solution)/shard_map/all_to_all | solution.py:166
Sparse Core Ops, SparseCore 0:
  9.9 31.1 all-gather.1
  263.8 38.8 reduce-scatter.1
  305.0 35.4 all-reduce.2
where the time goes:
time: 361 us; the launch traced here: 360 us
  matrix products  167 us (46%)
  waiting for transfers between devices  53.5 us (15%)
  blocking collectives  41.4 us (11%)
  other arithmetic  33.4 us (9%)
  local copies, waits for them, and re-layouts  19.5 us (5%)
  starting transfers between devices  18.9 us (5%)
  between operations  14.7 us (4%)
  loops' own time  12.3 us (3%)
    dot_general x16, matrix products, render_rays(): jnp.dot(h_zero, w_first, preferred_element_type=jnp.float32) * fan_scale  73.2 us
    dot_general x16, matrix products, render_rays(): lax.dot_general(h_zero, d_aone, (((0,), (0,)), ((), ())), preferred_eleme...  67.2 us
    psum x1, blocking collectives, body(): lax.psum((gain_part, loss_sum), ('grp', 'shard'))  41.4 us
    reduce_scatter x1, waiting for transfers between devices, body(): lax.psum_scatter(lax.dot_general(columns, d_field, (((0,), (0,)), ((), ()...  38 us
    another operation x1, loops' own time, body(): lax.scan(render_block, (zero_grad, zero_grad, jnp.zeros((), jnp.float32))...  12.3 us
    reduce_sum x16, other arithmetic, render_rays(): jnp.sum(jnp.where(live_rays, jnp.sum(residual * residual, axis=0) * scene...  9.75 us
    all_to_all x1, starting transfers between devices, body(): lax.all_to_all(send_live, ('grp', 'shard'), split_axis=0, concat_axis=0,...  7.33 us
  transfers between devices with their start and end apart: 7, of which 5 were waited for; matrix products, arithmetic and copies ran while one was open for 4% of the time, Pallas kernels for 0%

commit v1 on v0

--- a/solution.py
+++ b/solution.py
@@ -187,7 +187,7 @@
     )
     head_grad = lax.psum(group_part, "grp").astype(jnp.float32)
     gain_part = jnp.sum(d_norm * x_hat, axis=0)
-    norm_gain_grad, loss_total = lax.psum((gain_part, loss_sum), ("grp", "shard"))
+    norm_gain_grad, loss_total = lax.psum(lax.psum((gain_part, loss_sum), "shard"), "grp")
     d_scaled = d_norm * norm_gain
     latent_grad = (
         inv_rms * (d_scaled - x_hat * jnp.mean(d_scaled * x_hat, axis=1, keepdims=True))

time: 361 us -> 349 us (0.967)
  blocking collectives: 41.4 us -> 28.4 us
    psum x1 -> x2, blocking collectives: 41.4 us -> 28.4 us  [the longest x1 15.9 us: body(): lax.psum((gain_part, loss_sum), 'shard')]
  transfers between devices with their start and end apart: 7 -> 7, of which waited for: 5 -> 6; matrix products, arithmetic and copies ran while one was open for 4% -> 5% of each run, Pallas kernels for 0% -> 0%
where the time goes in v1:
time: 349 us
  matrix products  167 us (48%)
  waiting for transfers between devices  55.1 us (16%)
  other arithmetic  33.4 us (10%)
  blocking collectives  28.4 us (8%)
  local copies, waits for them, and re-layouts  19.5 us (6%)
  starting transfers between devices  18.9 us (5%)
  between operations  14.7 us (4%)
  loops' own time  12.3 us (4%)
    dot_general x16, matrix products, render_rays(): jnp.dot(h_zero, w_first, preferred_element_type=jnp.float32) * fan_scale  73.2 us
    dot_general x16, matrix products, render_rays(): lax.dot_general(h_zero, d_aone, (((0,), (0,)), ((), ())), preferred_eleme...  67.2 us
    reduce_scatter x1, waiting for transfers between devices, body(): lax.psum_scatter(lax.dot_general(columns, d_field, (((0,), (0,)), ((), ()...  38 us
    psum x1, blocking collectives, body(): lax.psum((gain_part, loss_sum), 'shard')  15.9 us
    psum x1, blocking collectives, body(): lax.psum(lax.psum((gain_part, loss_sum), 'shard'), 'grp')  12.4 us
    another operation x1, loops' own time, body(): lax.scan(render_block, (zero_grad, zero_grad, jnp.zeros((), jnp.float32))...  12.3 us
    reduce_sum x16, other arithmetic, render_rays(): jnp.sum(jnp.where(live_rays, jnp.sum(residual * residual, axis=0) * scene...  9.75 us
    all_to_all x1, starting transfers between devices, body(): lax.all_to_all(send_live, ('grp', 'shard'), split_axis=0, concat_axis=0,...  7.33 us
  transfers between devices with their start and end apart: 7, of which 6 were waited for; matrix products, arithmetic and copies ran while one was open for 5% of the time, Pallas kernels for 0%

profile of v1, /device:TPU:0, one launch (start us, length us, event | category | flops | bytes accessed | tf_op | source)
XLA Modules:
  0.0 348.7 jit_solution(1366930259676103469)
XLA Ops:
  7.2 0.7 all-gather.2.cloned.1.call-update
  7.9 0.8 convert_reduce_fusion
  8.7 0.7 compare_select_fusion.5
  9.4 0.8 scatter_custom_fusion.1
  10.2 0.7 all_to_all.28
  10.9 7.3 %all-to-all-start.1 = ((f32[32,8,1]{1,2,0:T(1,128)}), f32[32,8,1]{1,2,0:T(1,128)S(1)}, u32[]{:S(2)}, u32[]{:S(2)}) async-start(f32[32,8,1]{1,2,0:T(1,128)} %bitcast.2), calls=%async_computation.1 | async-start | bytes 32768 | tf_op jit(solution)/shard_map/all_to_all | solution.py:131
  18.2 1.1 fusion.46
  19.3 0.8 copy.34
  20.1 0.8 scatter_custom_fusion.2
  20.9 0.9 copy.35
  21.8 1.9 scatter_custom_fusion
  23.6 1.7 all-to-all-done.1
  25.4 4.1 %all-to-all-start.2 = ((f32[32,8,3]{1,2,0:T(4,128)}), f32[32,8,3]{1,2,0:T(4,128)S(1)}, u32[]{:S(2)}, u32[]{:S(2)}) async-start(f32[32,8,3]{1,2,0:T(4,128)} %copy.35), calls=%async_computation.2 | async-start | bytes 131072 | tf_op jit(solution)/shard_map/all_to_all | solution.py:130
  30.0 1.3 fusion.59
  32.1 4.9 %all-to-all-done.2 = f32[32,8,3]{1,2,0:T(4,128)S(1)} async-done(((f32[32,8,3]{1,2,0:T(4,128)}), f32[32,8,3]{1,2,0:T(4,128)S(1)}, u32[]{:S(2)}, u32[]{:S(2)}) %all-to-all-start.2) | async-done | bytes 3104 | tf_op jit(solution)/shard_map/all_to_all | solution.py:130
  37.0 2.7 all-to-all-start
  39.9 1.2 all-gather.2.cloned.1.call-done
  41.1 2.1 convolution_convert_fusion.1
  43.4 6.9 %all-to-all-done = f32[32,8,256]{2,1,0:T(8,128)S(1)} async-done(((f32[32,8,256]{2,1,0:T(8,128)}), f32[32,8,256]{2,1,0:T(8,128)S(1)}, u32[]{:S(2)}, u32[]{:S(2)}) %all-to-all-start) | async-done | bytes 262176 | tf_op jit(solution)/shard_map/all_to_all | solution.py:129
  50.3 210.8 %while.20 = (s32[]{:T(128)}, f32[256,256]{1,0:T(8,128)S(1)}, f32[256,256]{1,0:T(8,128)S(1)}, f32[]{:T(128)}, f32[16,3,16]{2,1,0:T(4,128)S(1)}, /*index=5*/f32[16...) while((s32[]{:T(128)}, f32[256,256]{1,0:T(8,128)S(1)}, ...), condition=%wide.region_14.15_spmd.clone, body=%wide.region_6.14_spmd.clone.sunk | while | flops 683649216 | bytes 7148784 | solution.py:162
  50.6 4.6 %fusion.109 = bf16[1024,256]{1,0:T(8,128)(2,1)S(1)} fusion(bf16[256,256]{1,0:T(8,128)(2,1)S(1)} %get-tuple-element.518, f32[256]{0:T(256)S(1)} %get-tuple-element.467, f32[256]{0:T(256)S(1)} %get-tuple-element.468, f32[256]{0:T(256)S(1)} %get-tuple-element.469, f32[1024]{0:T(1024)S(1)} %bitcast.98, f32[256]{0:T(256)S(1)} %get-tuple-element.471, ...), kind=kOutput, calls=%fused_computation.12.clone.1 | convolution fusion | flops 137101312 | bytes 672768 | tf_op jit(solution)/shard_map/while/body/eval_jaxpr/dot_general | solution.py:39
  56.3 0.6 select_reduce_fusion.2
  58.6 4.2 %fusion.114 = f32[256,256]{1,0:T(8,128)S(1)} fusion(bf16[1024,256]{1,0:T(8,128)(2,1)S(1)} %fusion.113, bf16[256,256]{1,0:T(8,128)(2,1)S(1)} %get-tuple-element.519, bf16[1024,256]{1,0:T(8,128)(2,1)S(1)} %fusion.109, f32[256,256]{1,0:T(8,128)S(1)} %get-tuple-element.497, f32[256]{0:T(256)S(1)} %get-tuple-element.467, f32[256]{0:T(256)S(1)} %get-tuple-element.468, ...), kind=kOutput, calls=%fused_computation.17.clone.1 | convolution fusion | flops 271712256 | bytes 1721345 | tf_op jit(solution)/shard_map/while/body/eval_jaxpr/dot_general | solution.py:81
  63.7 4.6 %fusion.109 = bf16[1024,256]{1,0:T(8,128)(2,1)S(1)} fusion(bf16[256,256]{1,0:T(8,128)(2,1)S(1)} %get-tuple-element.518, f32[256]{0:T(256)S(1)} %get-tuple-element.467, f32[256]{0:T(256)S(1)} %get-tuple-element.468, f32[256]{0:T(256)S(1)} %get-tuple-element.469, f32[1024]{0:T(1024)S(1)} %bitcast.98, f32[256]{0:T(256)S(1)} %get-tuple-element.471, ...), kind=kOutput, calls=%fused_computation.12.clone.1 | convolution fusion | flops 137101312 | bytes 672768 | tf_op jit(solution)/shard_map/while/body/eval_jaxpr/dot_general | solution.py:39
  71.8 4.2 %fusion.114 = f32[256,256]{1,0:T(8,128)S(1)} fusion(bf16[1024,256]{1,0:T(8,128)(2,1)S(1)} %fusion.113, bf16[256,256]{1,0:T(8,128)(2,1)S(1)} %get-tuple-element.519, bf16[1024,256]{1,0:T(8,128)(2,1)S(1)} %fusion.109, f32[256,256]{1,0:T(8,128)S(1)} %get-tuple-element.497, f32[256]{0:T(256)S(1)} %get-tuple-element.467, f32[256]{0:T(256)S(1)} %get-tuple-element.468, ...), kind=kOutput, calls=%fused_computation.17.clone.1 | convolution fusion | flops 271712256 | bytes 1721345 | tf_op jit(solution)/shard_map/while/body/eval_jaxpr/dot_general | solution.py:81
  76.9 4.6 %fusion.109 = bf16[1024,256]{1,0:T(8,128)(2,1)S(1)} fusion(bf16[256,256]{1,0:T(8,128)(2,1)S(1)} %get-tuple-element.518, f32[256]{0:T(256)S(1)} %get-tuple-element.467, f32[256]{0:T(256)S(1)} %get-tuple-element.468, f32[256]{0:T(256)S(1)} %get-tuple-element.469, f32[1024]{0:T(1024)S(1)} %bitcast.98, f32[256]{0:T(256)S(1)} %get-tuple-element.471, ...), kind=kOutput, calls=%fused_computation.12.clone.1 | convolution fusion | flops 137101312 | bytes 672768 | tf_op jit(solution)/shard_map/while/body/eval_jaxpr/dot_general | solution.py:39
  84.9 4.2 %fusion.114 = f32[256,256]{1,0:T(8,128)S(1)} fusion(bf16[1024,256]{1,0:T(8,128)(2,1)S(1)} %fusion.113, bf16[256,256]{1,0:T(8,128)(2,1)S(1)} %get-tuple-element.519, bf16[1024,256]{1,0:T(8,128)(2,1)S(1)} %fusion.109, f32[256,256]{1,0:T(8,128)S(1)} %get-tuple-element.497, f32[256]{0:T(256)S(1)} %get-tuple-element.467, f32[256]{0:T(256)S(1)} %get-tuple-element.468, ...), kind=kOutput, calls=%fused_computation.17.clone.1 | convolution fusion | flops 271712256 | bytes 1721345 | tf_op jit(solution)/shard_map/while/body/eval_jaxpr/dot_general | solution.py:81
  90.1 4.6 %fusion.109 = bf16[1024,256]{1,0:T(8,128)(2,1)S(1)} fusion(bf16[256,256]{1,0:T(8,128)(2,1)S(1)} %get-tuple-element.518, f32[256]{0:T(256)S(1)} %get-tuple-element.467, f32[256]{0:T(256)S(1)} %get-tuple-element.468, f32[256]{0:T(256)S(1)} %get-tuple-element.469, f32[1024]{0:T(1024)S(1)} %bitcast.98, f32[256]{0:T(256)S(1)} %get-tuple-element.471, ...), kind=kOutput, calls=%fused_computation.12.clone.1 | convolution fusion | flops 137101312 | bytes 672768 | tf_op jit(solution)/shard_map/while/body/eval_jaxpr/dot_general | solution.py:39
  98.1 4.2 %fusion.114 = f32[256,256]{1,0:T(8,128)S(1)} fusion(bf16[1024,256]{1,0:T(8,128)(2,1)S(1)} %fusion.113, bf16[256,256]{1,0:T(8,128)(2,1)S(1)} %get-tuple-element.519, bf16[1024,256]{1,0:T(8,128)(2,1)S(1)} %fusion.109, f32[256,256]{1,0:T(8,128)S(1)} %get-tuple-element.497, f32[256]{0:T(256)S(1)} %get-tuple-element.467, f32[256]{0:T(256)S(1)} %get-tuple-element.468, ...), kind=kOutput, calls=%fused_computation.17.clone.1 | convolution fusion | flops 271712256 | bytes 1721345 | tf_op jit(solution)/shard_map/while/body/eval_jaxpr/dot_general | solution.py:81
  103.3 4.6 %fusion.109 = bf16[1024,256]{1,0:T(8,128)(2,1)S(1)} fusion(bf16[256,256]{1,0:T(8,128)(2,1)S(1)} %get-tuple-element.518, f32[256]{0:T(256)S(1)} %get-tuple-element.467, f32[256]{0:T(256)S(1)} %get-tuple-element.468, f32[256]{0:T(256)S(1)} %get-tuple-element.469, f32[1024]{0:T(1024)S(1)} %bitcast.98, f32[256]{0:T(256)S(1)} %get-tuple-element.471, ...), kind=kOutput, calls=%fused_computation.12.clone.1 | convolution fusion | flops 137101312 | bytes 672768 | tf_op jit(solution)/shard_map/while/body/eval_jaxpr/dot_general | solution.py:39
  111.3 4.2 %fusion.114 = f32[256,256]{1,0:T(8,128)S(1)} fusion(bf16[1024,256]{1,0:T(8,128)(2,1)S(1)} %fusion.113, bf16[256,256]{1,0:T(8,128)(2,1)S(1)} %get-tuple-element.519, bf16[1024,256]{1,0:T(8,128)(2,1)S(1)} %fusion.109, f32[256,256]{1,0:T(8,128)S(1)} %get-tuple-element.497, f32[256]{0:T(256)S(1)} %get-tuple-element.467, f32[256]{0:T(256)S(1)} %get-tuple-element.468, ...), kind=kOutput, calls=%fused_computation.17.clone.1 | convolution fusion | flops 271712256 | bytes 1721345 | tf_op jit(solution)/shard_map/while/body/eval_jaxpr/dot_general | solution.py:81
  116.5 4.6 %fusion.109 = bf16[1024,256]{1,0:T(8,128)(2,1)S(1)} fusion(bf16[256,256]{1,0:T(8,128)(2,1)S(1)} %get-tuple-element.518, f32[256]{0:T(256)S(1)} %get-tuple-element.467, f32[256]{0:T(256)S(1)} %get-tuple-element.468, f32[256]{0:T(256)S(1)} %get-tuple-element.469, f32[1024]{0:T(1024)S(1)} %bitcast.98, f32[256]{0:T(256)S(1)} %get-tuple-element.471, ...), kind=kOutput, calls=%fused_computation.12.clone.1 | convolution fusion | flops 137101312 | bytes 672768 | tf_op jit(solution)/shard_map/while/body/eval_jaxpr/dot_general | solution.py:39
  124.5 4.2 %fusion.114 = f32[256,256]{1,0:T(8,128)S(1)} fusion(bf16[1024,256]{1,0:T(8,128)(2,1)S(1)} %fusion.113, bf16[256,256]{1,0:T(8,128)(2,1)S(1)} %get-tuple-element.519, bf16[1024,256]{1,0:T(8,128)(2,1)S(1)} %fusion.109, f32[256,256]{1,0:T(8,128)S(1)} %get-tuple-element.497, f32[256]{0:T(256)S(1)} %get-tuple-element.467, f32[256]{0:T(256)S(1)} %get-tuple-element.468, ...), kind=kOutput, calls=%fused_computation.17.clone.1 | convolution fusion | flops 271712256 | bytes 1721345 | tf_op jit(solution)/shard_map/while/body/eval_jaxpr/dot_general | solution.py:81
  129.6 4.6 %fusion.109 = bf16[1024,256]{1,0:T(8,128)(2,1)S(1)} fusion(bf16[256,256]{1,0:T(8,128)(2,1)S(1)} %get-tuple-element.518, f32[256]{0:T(256)S(1)} %get-tuple-element.467, f32[256]{0:T(256)S(1)} %get-tuple-element.468, f32[256]{0:T(256)S(1)} %get-tuple-element.469, f32[1024]{0:T(1024)S(1)} %bitcast.98, f32[256]{0:T(256)S(1)} %get-tuple-element.471, ...), kind=kOutput, calls=%fused_computation.12.clone.1 | convolution fusion | flops 137101312 | bytes 672768 | tf_op jit(solution)/shard_map/while/body/eval_jaxpr/dot_general | solution.py:39
  137.7 4.2 %fusion.114 = f32[256,256]{1,0:T(8,128)S(1)} fusion(bf16[1024,256]{1,0:T(8,128)(2,1)S(1)} %fusion.113, bf16[256,256]{1,0:T(8,128)(2,1)S(1)} %get-tuple-element.519, bf16[1024,256]{1,0:T(8,128)(2,1)S(1)} %fusion.109, f32[256,256]{1,0:T(8,128)S(1)} %get-tuple-element.497, f32[256]{0:T(256)S(1)} %get-tuple-element.467, f32[256]{0:T(256)S(1)} %get-tuple-element.468, ...), kind=kOutput, calls=%fused_computation.17.clone.1 | convolution fusion | flops 271712256 | bytes 1721345 | tf_op jit(solution)/shard_map/while/body/eval_jaxpr/dot_general | solution.py:81
  142.8 4.6 %fusion.109 = bf16[1024,256]{1,0:T(8,128)(2,1)S(1)} fusion(bf16[256,256]{1,0:T(8,128)(2,1)S(1)} %get-tuple-element.518, f32[256]{0:T(256)S(1)} %get-tuple-element.467, f32[256]{0:T(256)S(1)} %get-tuple-element.468, f32[256]{0:T(256)S(1)} %get-tuple-element.469, f32[1024]{0:T(1024)S(1)} %bitcast.98, f32[256]{0:T(256)S(1)} %get-tuple-element.471, ...), kind=kOutput, calls=%fused_computation.12.clone.1 | convolution fusion | flops 137101312 | bytes 672768 | tf_op jit(solution)/shard_map/while/body/eval_jaxpr/dot_general | solution.py:39
  150.8 4.2 %fusion.114 = f32[256,256]{1,0:T(8,128)S(1)} fusion(bf16[1024,256]{1,0:T(8,128)(2,1)S(1)} %fusion.113, bf16[256,256]{1,0:T(8,128)(2,1)S(1)} %get-tuple-element.519, bf16[1024,256]{1,0:T(8,128)(2,1)S(1)} %fusion.109, f32[256,256]{1,0:T(8,128)S(1)} %get-tuple-element.497, f32[256]{0:T(256)S(1)} %get-tuple-element.467, f32[256]{0:T(256)S(1)} %get-tuple-element.468, ...), kind=kOutput, calls=%fused_computation.17.clone.1 | convolution fusion | flops 271712256 | bytes 1721345 | tf_op jit(solution)/shard_map/while/body/eval_jaxpr/dot_general | solution.py:81
  156.0 4.6 %fusion.109 = bf16[1024,256]{1,0:T(8,128)(2,1)S(1)} fusion(bf16[256,256]{1,0:T(8,128)(2,1)S(1)} %get-tuple-element.518, f32[256]{0:T(256)S(1)} %get-tuple-element.467, f32[256]{0:T(256)S(1)} %get-tuple-element.468, f32[256]{0:T(256)S(1)} %get-tuple-element.469, f32[1024]{0:T(1024)S(1)} %bitcast.98, f32[256]{0:T(256)S(1)} %get-tuple-element.471, ...), kind=kOutput, calls=%fused_computation.12.clone.1 | convolution fusion | flops 137101312 | bytes 672768 | tf_op jit(solution)/shard_map/while/body/eval_jaxpr/dot_general | solution.py:39
  164.0 4.2 %fusion.114 = f32[256,256]{1,0:T(8,128)S(1)} fusion(bf16[1024,256]{1,0:T(8,128)(2,1)S(1)} %fusion.113, bf16[256,256]{1,0:T(8,128)(2,1)S(1)} %get-tuple-element.519, bf16[1024,256]{1,0:T(8,128)(2,1)S(1)} %fusion.109, f32[256,256]{1,0:T(8,128)S(1)} %get-tuple-element.497, f32[256]{0:T(256)S(1)} %get-tuple-element.467, f32[256]{0:T(256)S(1)} %get-tuple-element.468, ...), kind=kOutput, calls=%fused_computation.17.clone.1 | convolution fusion | flops 271712256 | bytes 1721345 | tf_op jit(solution)/shard_map/while/body/eval_jaxpr/dot_general | solution.py:81
  169.2 4.6 %fusion.109 = bf16[1024,256]{1,0:T(8,128)(2,1)S(1)} fusion(bf16[256,256]{1,0:T(8,128)(2,1)S(1)} %get-tuple-element.518, f32[256]{0:T(256)S(1)} %get-tuple-element.467, f32[256]{0:T(256)S(1)} %get-tuple-element.468, f32[256]{0:T(256)S(1)} %get-tuple-element.469, f32[1024]{0:T(1024)S(1)} %bitcast.98, f32[256]{0:T(256)S(1)} %get-tuple-element.471, ...), kind=kOutput, calls=%fused_computation.12.clone.1 | convolution fusion | flops 137101312 | bytes 672768 | tf_op jit(solution)/shard_map/while/body/eval_jaxpr/dot_general | solution.py:39
  177.2 4.2 %fusion.114 = f32[256,256]{1,0:T(8,128)S(1)} fusion(bf16[1024,256]{1,0:T(8,128)(2,1)S(1)} %fusion.113, bf16[256,256]{1,0:T(8,128)(2,1)S(1)} %get-tuple-element.519, bf16[1024,256]{1,0:T(8,128)(2,1)S(1)} %fusion.109, f32[256,256]{1,0:T(8,128)S(1)} %get-tuple-element.497, f32[256]{0:T(256)S(1)} %get-tuple-element.467, f32[256]{0:T(256)S(1)} %get-tuple-element.468, ...), kind=kOutput, calls=%fused_computation.17.clone.1 | convolution fusion | flops 271712256 | bytes 1721345 | tf_op jit(solution)/shard_map/while/body/eval_jaxpr/dot_general | solution.py:81
  182.4 4.6 %fusion.109 = bf16[1024,256]{1,0:T(8,128)(2,1)S(1)} fusion(bf16[256,256]{1,0:T(8,128)(2,1)S(1)} %get-tuple-element.518, f32[256]{0:T(256)S(1)} %get-tuple-element.467, f32[256]{0:T(256)S(1)} %get-tuple-element.468, f32[256]{0:T(256)S(1)} %get-tuple-element.469, f32[1024]{0:T(1024)S(1)} %bitcast.98, f32[256]{0:T(256)S(1)} %get-tuple-element.471, ...), kind=kOutput, calls=%fused_computation.12.clone.1 | convolution fusion | flops 137101312 | bytes 672768 | tf_op jit(solution)/shard_map/while/body/eval_jaxpr/dot_general | solution.py:39
  190.4 4.2 %fusion.114 = f32[256,256]{1,0:T(8,128)S(1)} fusion(bf16[1024,256]{1,0:T(8,128)(2,1)S(1)} %fusion.113, bf16[256,256]{1,0:T(8,128)(2,1)S(1)} %get-tuple-element.519, bf16[1024,256]{1,0:T(8,128)(2,1)S(1)} %fusion.109, f32[256,256]{1,0:T(8,128)S(1)} %get-tuple-element.497, f32[256]{0:T(256)S(1)} %get-tuple-element.467, f32[256]{0:T(256)S(1)} %get-tuple-element.468, ...), kind=kOutput, calls=%fused_computation.17.clone.1 | convolution fusion | flops 271712256 | bytes 1721345 | tf_op jit(solution)/shard_map/while/body/eval_jaxpr/dot_general | solution.py:81
  195.5 4.6 %fusion.109 = bf16[1024,256]{1,0:T(8,128)(2,1)S(1)} fusion(bf16[256,256]{1,0:T(8,128)(2,1)S(1)} %get-tuple-element.518, f32[256]{0:T(256)S(1)} %get-tuple-element.467, f32[256]{0:T(256)S(1)} %get-tuple-element.468, f32[256]{0:T(256)S(1)} %get-tuple-element.469, f32[1024]{0:T(1024)S(1)} %bitcast.98, f32[256]{0:T(256)S(1)} %get-tuple-element.471, ...), kind=kOutput, calls=%fused_computation.12.clone.1 | convolution fusion | flops 137101312 | bytes 672768 | tf_op jit(solution)/shard_map/while/body/eval_jaxpr/dot_general | solution.py:39
  203.6 4.2 %fusion.114 = f32[256,256]{1,0:T(8,128)S(1)} fusion(bf16[1024,256]{1,0:T(8,128)(2,1)S(1)} %fusion.113, bf16[256,256]{1,0:T(8,128)(2,1)S(1)} %get-tuple-element.519, bf16[1024,256]{1,0:T(8,128)(2,1)S(1)} %fusion.109, f32[256,256]{1,0:T(8,128)S(1)} %get-tuple-element.497, f32[256]{0:T(256)S(1)} %get-tuple-element.467, f32[256]{0:T(256)S(1)} %get-tuple-element.468, ...), kind=kOutput, calls=%fused_computation.17.clone.1 | convolution fusion | flops 271712256 | bytes 1721345 | tf_op jit(solution)/shard_map/while/body/eval_jaxpr/dot_general | solution.py:81
  208.7 4.6 %fusion.109 = bf16[1024,256]{1,0:T(8,128)(2,1)S(1)} fusion(bf16[256,256]{1,0:T(8,128)(2,1)S(1)} %get-tuple-element.518, f32[256]{0:T(256)S(1)} %get-tuple-element.467, f32[256]{0:T(256)S(1)} %get-tuple-element.468, f32[256]{0:T(256)S(1)} %get-tuple-element.469, f32[1024]{0:T(1024)S(1)} %bitcast.98, f32[256]{0:T(256)S(1)} %get-tuple-element.471, ...), kind=kOutput, calls=%fused_computation.12.clone.1 | convolution fusion | flops 137101312 | bytes 672768 | tf_op jit(solution)/shard_map/while/body/eval_jaxpr/dot_general | solution.py:39
  216.7 4.2 %fusion.114 = f32[256,256]{1,0:T(8,128)S(1)} fusion(bf16[1024,256]{1,0:T(8,128)(2,1)S(1)} %fusion.113, bf16[256,256]{1,0:T(8,128)(2,1)S(1)} %get-tuple-element.519, bf16[1024,256]{1,0:T(8,128)(2,1)S(1)} %fusion.109, f32[256,256]{1,0:T(8,128)S(1)} %get-tuple-element.497, f32[256]{0:T(256)S(1)} %get-tuple-element.467, f32[256]{0:T(256)S(1)} %get-tuple-element.468, ...), kind=kOutput, calls=%fused_computation.17.clone.1 | convolution fusion | flops 271712256 | bytes 1721345 | tf_op jit(solution)/shard_map/while/body/eval_jaxpr/dot_general | solution.py:81
  221.9 4.6 %fusion.109 = bf16[1024,256]{1,0:T(8,128)(2,1)S(1)} fusion(bf16[256,256]{1,0:T(8,128)(2,1)S(1)} %get-tuple-element.518, f32[256]{0:T(256)S(1)} %get-tuple-element.467, f32[256]{0:T(256)S(1)} %get-tuple-element.468, f32[256]{0:T(256)S(1)} %get-tuple-element.469, f32[1024]{0:T(1024)S(1)} %bitcast.98, f32[256]{0:T(256)S(1)} %get-tuple-element.471, ...), kind=kOutput, calls=%fused_computation.12.clone.1 | convolution fusion | flops 137101312 | bytes 672768 | tf_op jit(solution)/shard_map/while/body/eval_jaxpr/dot_general | solution.py:39
  229.9 4.2 %fusion.114 = f32[256,256]{1,0:T(8,128)S(1)} fusion(bf16[1024,256]{1,0:T(8,128)(2,1)S(1)} %fusion.113, bf16[256,256]{1,0:T(8,128)(2,1)S(1)} %get-tuple-element.519, bf16[1024,256]{1,0:T(8,128)(2,1)S(1)} %fusion.109, f32[256,256]{1,0:T(8,128)S(1)} %get-tuple-element.497, f32[256]{0:T(256)S(1)} %get-tuple-element.467, f32[256]{0:T(256)S(1)} %get-tuple-element.468, ...), kind=kOutput, calls=%fused_computation.17.clone.1 | convolution fusion | flops 271712256 | bytes 1721345 | tf_op jit(solution)/shard_map/while/body/eval_jaxpr/dot_general | solution.py:81
  235.1 4.6 %fusion.109 = bf16[1024,256]{1,0:T(8,128)(2,1)S(1)} fusion(bf16[256,256]{1,0:T(8,128)(2,1)S(1)} %get-tuple-element.518, f32[256]{0:T(256)S(1)} %get-tuple-element.467, f32[256]{0:T(256)S(1)} %get-tuple-element.468, f32[256]{0:T(256)S(1)} %get-tuple-element.469, f32[1024]{0:T(1024)S(1)} %bitcast.98, f32[256]{0:T(256)S(1)} %get-tuple-element.471, ...), kind=kOutput, calls=%fused_computation.12.clone.1 | convolution fusion | flops 137101312 | bytes 672768 | tf_op jit(solution)/shard_map/while/body/eval_jaxpr/dot_general | solution.py:39
  243.1 4.2 %fusion.114 = f32[256,256]{1,0:T(8,128)S(1)} fusion(bf16[1024,256]{1,0:T(8,128)(2,1)S(1)} %fusion.113, bf16[256,256]{1,0:T(8,128)(2,1)S(1)} %get-tuple-element.519, bf16[1024,256]{1,0:T(8,128)(2,1)S(1)} %fusion.109, f32[256,256]{1,0:T(8,128)S(1)} %get-tuple-element.497, f32[256]{0:T(256)S(1)} %get-tuple-element.467, f32[256]{0:T(256)S(1)} %get-tuple-element.468, ...), kind=kOutput, calls=%fused_computation.17.clone.1 | convolution fusion | flops 271712256 | bytes 1721345 | tf_op jit(solution)/shard_map/while/body/eval_jaxpr/dot_general | solution.py:81
  248.2 4.6 %fusion.109 = bf16[1024,256]{1,0:T(8,128)(2,1)S(1)} fusion(bf16[256,256]{1,0:T(8,128)(2,1)S(1)} %get-tuple-element.518, f32[256]{0:T(256)S(1)} %get-tuple-element.467, f32[256]{0:T(256)S(1)} %get-tuple-element.468, f32[256]{0:T(256)S(1)} %get-tuple-element.469, f32[1024]{0:T(1024)S(1)} %bitcast.98, f32[256]{0:T(256)S(1)} %get-tuple-element.471, ...), kind=kOutput, calls=%fused_computation.12.clone.1 | convolution fusion | flops 137101312 | bytes 672768 | tf_op jit(solution)/shard_map/while/body/eval_jaxpr/dot_general | solution.py:39
  256.3 4.2 %fusion.114 = f32[256,256]{1,0:T(8,128)S(1)} fusion(bf16[1024,256]{1,0:T(8,128)(2,1)S(1)} %fusion.113, bf16[256,256]{1,0:T(8,128)(2,1)S(1)} %get-tuple-element.519, bf16[1024,256]{1,0:T(8,128)(2,1)S(1)} %fusion.109, f32[256,256]{1,0:T(8,128)S(1)} %get-tuple-element.497, f32[256]{0:T(256)S(1)} %get-tuple-element.467, f32[256]{0:T(256)S(1)} %get-tuple-element.468, ...), kind=kOutput, calls=%fused_computation.17.clone.1 | convolution fusion | flops 271712256 | bytes 1721345 | tf_op jit(solution)/shard_map/while/body/eval_jaxpr/dot_general | solution.py:81
  261.4 2.1 convolution_convert_fusion
  263.7 0.9 fusion.42
  264.6 38.0 %reduce-scatter.2.cloned.1.call-done = bf16[128,1024]{1,0:T(8,128)(2,1)} async-done(((bf16[1024,1024]{1,0:T(8,128)(2,1)}), bf16[128,1024]{1,0:T(8,128)(2,1)}) %reduce-scatter.2.cloned.1.call-update) | async-done | bytes 262160 | tf_op jit(solution)/shard_map/reduce_scatter | solution.py:180
  302.7 0.7 copy.39
  303.3 4.6 %all-to-all-start.3 = ((f32[3,32,8]{2,0,1:T(4,128)}), f32[3,32,8]{2,0,1:T(4,128)S(1)}, u32[]{:S(2)}, u32[]{:S(2)}) async-start(f32[3,32,8]{2,0,1:T(4,128)} %copy.39), calls=%async_computation.3 | async-start | bytes 131072 | tf_op jit(solution)/shard_map/all_to_all | solution.py:166
  308.0 0.9 fusion.45
  308.9 15.9 %all-reduce = (f32[]{:T(128)}, f32[1024]{0:T(1024)S(1)}) all-reduce(f32[]{:T(128)} %get-tuple-element.221, f32[1024]{0:T(1024)S(1)} %get-tuple-element.326), channel_id=1, replica_groups=mesh['grp'=4,'shard'=8] {'shard'}, use_global_device_ids=true, to_apply=%region_15.16 | all-reduce | flops 1025 | bytes 8200 | tf_op jit(solution)/shard_map/psum | solution.py:190
  324.8 12.4 %all-reduce.1 = (f32[]{:T(128)}, f32[1024]{0:T(1024)}) all-reduce(f32[]{:T(128)} %get-tuple-element.355, f32[1024]{0:T(1024)S(1)} %get-tuple-element.356), channel_id=1, replica_groups=mesh['grp'=4,'shard'=8] {'grp'}, use_global_device_ids=true, to_apply=%region_16.17 | all-reduce | flops 1025 | bytes 8200 | tf_op jit(solution)/shard_map/psum | solution.py:190
  338.1 0.7 copy.41
  338.8 1.6 all-reduce.4.cloned.1.call-done
  340.4 1.8 convert_element_type.122
  (581 shorter events, 59.8 us)
Async XLA Ops:
  7.2 33.9 %copy-start.1 = (bf16[128,1024]{1,0:T(8,128)(2,1)S(1)}, bf16[128,1024]{1,0:T(8,128)(2,1)}, u32[]{:S(2)}) copy-start(bf16[128,1024]{1,0:T(8,128)(2,1)} %param.10) | copy-start | bytes 786436
  7.2 33.9 %copy-start.2 = (f32[1024]{0:T(1024)S(1)}, f32[1024]{0:T(1024)}, u32[]{:S(2)}) copy-start(f32[1024]{0:T(1024)} %param.12) | copy-start | bytes 12292
  7.2 33.9 %all-gather.2.cloned.1.call-start = ((), (), s32[]{:S(2)}) async-start(), calls=%async_computation.5 | async-start | bytes 2359296 | tf_op jit(solution)/shard_map/all_gather | solution.py:111
  10.9 14.5 %all-to-all-start.1 = ((f32[32,8,1]{1,2,0:T(1,128)}), f32[32,8,1]{1,2,0:T(1,128)S(1)}, u32[]{:S(2)}, u32[]{:S(2)}) async-start(f32[32,8,1]{1,2,0:T(1,128)} %bitcast.2), calls=%async_computation.1 | async-start | bytes 32768 | tf_op jit(solution)/shard_map/all_to_all | solution.py:131
  25.4 11.6 %all-to-all-start.2 = ((f32[32,8,3]{1,2,0:T(4,128)}), f32[32,8,3]{1,2,0:T(4,128)S(1)}, u32[]{:S(2)}, u32[]{:S(2)}) async-start(f32[32,8,3]{1,2,0:T(4,128)} %copy.35), calls=%async_computation.2 | async-start | bytes 131072 | tf_op jit(solution)/shard_map/all_to_all | solution.py:130
  37.0 13.3 %copy-start.3 = (bf16[4,256]{1,0:T(4,128)(2,1)S(1)}, bf16[4,256]{1,0:T(4,128)(2,1)}, u32[]{:S(2)}) copy-start(bf16[4,256]{1,0:T(4,128)(2,1)} %param.13) | copy-start | bytes 6148
  37.0 13.3 %all-to-all-start = ((f32[32,8,256]{2,1,0:T(8,128)}), f32[32,8,256]{2,1,0:T(8,128)S(1)}, u32[]{:S(2)}, u32[]{:S(2)}) async-start(f32[32,8,256]{2,1,0:T(8,128)} %bitcast), calls=%async_computation | async-start | bytes 524288 | tf_op jit(solution)/shard_map/all_to_all | solution.py:129
  39.7 262.8 %reduce-scatter.2.cloned.1.call-start = ((), (), s32[]{:S(2)}) async-start(), calls=%async_computation.6 | async-start | bytes 2359296 | tf_op jit(solution)/shard_map/reduce_scatter | solution.py:180
  261.4 2.2 copy-start
  263.6 76.8 %all-reduce.4.cloned.1.call-start = ((), (), s32[]{:S(2)}) async-start(), calls=%async_computation.7 | async-start | bytes 524288 | tf_op jit(solution)/shard_map/psum | solution.py:188
  303.3 33.9 %all-to-all-start.3 = ((f32[3,32,8]{2,0,1:T(4,128)}), f32[3,32,8]{2,0,1:T(4,128)S(1)}, u32[]{:S(2)}, u32[]{:S(2)}) async-start(f32[3,32,8]{2,0,1:T(4,128)} %copy.39), calls=%async_computation.3 | async-start | bytes 131072 | tf_op jit(solution)/shard_map/all_to_all | solution.py:166
Sparse Core Ops, SparseCore 0:
  9.9 31.1 all-gather.1
  263.7 38.8 reduce-scatter.1
  304.9 35.4 all-reduce.3
